TPU v7x, 256 devices: a whole 4x4x8 slice. The times are simulated.
256 devices in a mesh: occ: 8 (over y_lo, x), vir: 32 (over y_hi, z, core).
Axes of the slice: x: 4, y: 4 (y_hi: 2, y_lo: 2; y = y_hi * 2 + y_lo), z: 8, core: 2. Of those that a mesh axis runs over, the one named last changes fastest.
Arguments:
- factors: bfloat16 [256, 1024, 2048], P(None, 'vir', 'occ'), may hold values from -0.125 to 0.125
- e_occ: float32 [256], replicated, may hold values from -2 to -0.3
- e_vir: float32 [1024], replicated, may hold values from 0.1 to 3
- i_sub: int32 [3], replicated, may hold values from 0 to 1
- j_row: int32 [3], replicated, may hold values from 0 to 255
Outputs:
- density: float32 [256, 1024, 2048], P(None, 'vir', 'occ')
All inputs are finite; a program needn't handle non-finite values.
Results may differ from a plain program's by a relative error of at most 0.0022.
Values may be sent and summed in bfloat16 or wider, within the bound.
A program may use at most 128 MiB of HBM per device.

v0:
```python
import jax
import jax.numpy as jnp
from jax import lax
from jax.sharding import PartitionSpec as P

IBK = 16
STEPS = 3


def from_root(shard, axis, root):
    mine = lax.axis_index(axis) == root
    return lax.psum(jnp.where(mine, shard, jnp.zeros_like(shard)), axis)


def pair_terms(accumulator, row_block, energy_rows, energy_own, energy_pair, column_piece, e_vir):
    integrals = jnp.einsum(
        "iap,bp->iab", row_block, column_piece, preferred_element_type=jnp.float32
    )
    denominator = (
        energy_own[None, :, None] + e_vir[None, None, :] - energy_rows[:, None, None] - energy_pair
    )
    amplitude = (-integrals / denominator).astype(jnp.bfloat16)
    return accumulator + jnp.einsum(
        "iab,bp->iap", amplitude, column_piece, preferred_element_type=jnp.float32
    )


def shards(factors, e_occ, e_vir, i_sub, j_row):
    regrouped = lax.all_to_all(factors, "occ", split_axis=0, concat_axis=2, tiled=True)
    owned, vir_own, aux_total = regrouped.shape
    occ_rank = lax.axis_index("occ")
    vir_rank = lax.axis_index("vir")
    energy_own = lax.dynamic_slice_in_dim(e_vir, vir_rank * vir_own, vir_own, 0)
    density = jnp.zeros((owned, vir_own, aux_total), jnp.float32)
    offsets = []
    row_blocks = []
    energy_list = []
    pair_slabs = []
    pair_energies = []
    for step_index in range(STEPS):
        offset = i_sub[step_index] * IBK
        j_index = j_row[step_index]
        owner = j_index // owned
        own_slab = lax.dynamic_index_in_dim(regrouped, j_index % owned, 0, keepdims=False)
        pair_slab = from_root(own_slab, "occ", owner)
        offsets.append(offset)
        row_blocks.append(lax.dynamic_slice_in_dim(regrouped, offset, IBK, 0))
        energy_list.append(lax.dynamic_slice_in_dim(e_occ, occ_rank * owned + offset, IBK, 0))
        pair_slabs.append(pair_slab)
        pair_energies.append(e_occ[j_index])
    for step_index in range(STEPS):
        previous = lax.dynamic_slice_in_dim(density, offsets[step_index], IBK, 0)
        updated = pair_terms(
            previous,
            row_blocks[step_index],
            energy_list[step_index],
            energy_own,
            pair_energies[step_index],
            lax.all_gather(pair_slabs[step_index], "vir", axis=0, tiled=True),
            e_vir,
        )
        density = lax.dynamic_update_slice_in_dim(density, updated, offsets[step_index], 0)
    return lax.all_to_all(density, "occ", split_axis=2, concat_axis=0, tiled=True)


def solution(mesh):
    placed = (P(None, "vir", "occ"), P(), P(), P(), P())
    return jax.shard_map(
        shards, mesh=mesh, in_specs=placed, out_specs=P(None, "vir", "occ"), check_vma=False
    )
```

profile of v0, /device:TPU:1, one launch (start us, length us, event | category | flops | bytes accessed | tf_op | source)
XLA Modules:
  0.0 679.4 jit_solution(2114121080004834413)
XLA Ops:
  6.5 6.0 all-to-all-start
  12.6 0.6 fusion.64
  20.4 41.8 %all-to-all-done = bf16[256,32,256]{2,1,0:T(8,128)(2,1)} async-done(((bf16[256,32,256]{2,1,0:T(8,128)(2,1)}), bf16[256,32,256]{2,1,0:T(8,128)(2,1)}, u32[]{:S(2)}, u32[]{:S(2)}) %all-to-all-start) | async-done | bytes 4194336 | tf_op jit(solution)/shard_map/all_to_all | solution.py:29
  62.2 8.5 %copy.12 = bf16[8,32,32,256]{3,0,2,1:T(8,128)(2,1)} copy(bf16[8,32,32,256]{3,2,1,0:T(8,128)(2,1)} %bitcast) | data formatting | bytes 8388608 | tf_op jit(solution)/shard_map/all_to_all | solution.py:29
  70.7 7.4 %all_to_all.29 = bf16[32,32,2048]{2,1,0:T(8,128)(2,1)} reshape(bf16[32,32,8,256]{3,2,1,0:T(8,128)(2,1)} %bitcast.62) | data formatting | bytes 8388608 | tf_op jit(solution)/shard_map/all_to_all | solution.py:29
  78.1 1.8 select_bitcast_fusion
  80.0 89.0 %all-reduce.3.cloned.1.call-done = (bf16[32,2048]{1,0:T(8,128)(2,1)}, bf16[32,2048]{1,0:T(8,128)(2,1)}, bf16[32,2048]{1,0:T(8,128)(2,1)}) async-done(((bf16[32,2048]{1,0:T(8,128)(2,1)}, bf16[32,2048]{1,0:T(8,128)(2,1)}, bf16[32,2048]{1,0:T(8,128)(2,1)}), (bf16[32,2048]{1,0:T(8,128)(2,1)}, bf16[32,2048]{1,0:T(8,128)(2,1)}, bf16[32,2048]{1,0:T(8,128)(2,1)})) %all-reduce.3.cloned.1.call-update) | async-done | bytes 393232 | tf_op jit(solution)/shard_map/psum | solution.py:12
  169.1 0.7 all-gather.6.cloned.1.call-update
  170.3 0.7 fusion.63
  176.5 0.6 fusion.62
  177.3 86.9 %all-gather.4.cloned.1.call-done = bf16[1024,2048]{1,0:T(8,128)(2,1)} async-done(((bf16[32,2048]{1,0:T(8,128)(2,1)}), bf16[1024,2048]{1,0:T(8,128)(2,1)}) %all-gather.4.cloned.1.call-update) | async-done | bytes 4194320 | tf_op jit(solution)/shard_map/all_gather | solution.py:59
  264.1 4.5 broadcast_in_dim.2
  268.6 11.2 %fusion.12 = f32[32,32,2048]{2,1,0:T(8,128)} fusion(f32[32,32,2048]{2,1,0:T(8,128)} %broadcast_in_dim.2, s32[]{:T(128)S(6)} %select_n.99, bf16[1024,2048]{1,0:T(8,128)(2,1)} %all-gather.4.cloned.1.call-done, bf16[32,32,2048]{2,1,0:T(8,128)(2,1)} %all_to_all.29, f32[]{:T(128)} %bitcast.6, f32[16]{0:T(128)S(1)} %get-tuple-element.13, ...), kind=kOutput, calls=%fused_computation.15 | convolution fusion | flops 4297588736 | bytes 14812736 | tf_op jit(solution)/shard_map/iab,bp->iap/dot_general | solution.py:23
  279.8 70.5 %all-gather.6.cloned.1.call-done = bf16[1024,2048]{1,0:T(8,128)(2,1)} async-done(((bf16[32,2048]{1,0:T(8,128)(2,1)}), bf16[1024,2048]{1,0:T(8,128)(2,1)}) %all-gather.6.cloned.1.call-update) | async-done | bytes 4194320 | tf_op jit(solution)/shard_map/all_gather | solution.py:59
  350.2 12.4 %add_dynamic-update-slice_fusion.1 = f32[32,32,2048]{2,1,0:T(8,128)} fusion(f32[32,32,2048]{2,1,0:T(8,128)} %fusion.12, s32[]{:T(128)S(6)} %select_n.109, bf16[1024,2048]{1,0:T(8,128)(2,1)} %all-gather.6.cloned.1.call-done, bf16[32,32,2048]{2,1,0:T(8,128)(2,1)} %all_to_all.29, f32[]{:T(128)} %bitcast.11, f32[16]{0:T(128)S(1)} %get-tuple-element.12, ...), kind=kOutput, calls=%fused_computation.14 | convolution fusion | flops 4298637312 | bytes 19007040 | tf_op jit(solution)/shard_map/iab,bp->iap/dot_general | solution.py:23
  362.7 73.5 %all-gather.8.cloned.1.call-done = bf16[1024,2048]{1,0:T(8,128)(2,1)} async-done(((bf16[32,2048]{1,0:T(8,128)(2,1)}), bf16[1024,2048]{1,0:T(8,128)(2,1)}) %all-gather.8.cloned.1.call-update) | async-done | bytes 4194320 | tf_op jit(solution)/shard_map/all_gather | solution.py:59
  436.2 12.5 %add_dynamic-update-slice_fusion = f32[32,32,2048]{2,1,0:T(8,128)} fusion(f32[32,32,2048]{2,1,0:T(8,128)} %add_dynamic-update-slice_fusion.1, s32[]{:T(128)S(6)} %select_n.118, bf16[1024,2048]{1,0:T(8,128)(2,1)} %all-gather.8.cloned.1.call-done, bf16[32,32,2048]{2,1,0:T(8,128)(2,1)} %all_to_all.29, f32[]{:T(128)} %bitcast.16, f32[16]{0:T(128)S(1)} %get-tuple-element.11, ...), kind=kOutput, calls=%fused_computation.13 | convolution fusion | flops 4298637312 | bytes 19007040 | tf_op jit(solution)/shard_map/iab,bp->iap/dot_general | solution.py:23
  448.6 26.3 %copy.9 = f32[32,32,2048]{1,0,2:T(8,128)} copy(f32[32,32,2048]{2,1,0:T(8,128)} %add_dynamic-update-slice_fusion) | data formatting | bytes 16777216 | tf_op jit(solution)/shard_map/dynamic_update_slice | solution.py:62
  474.9 20.5 %reshape.53 = f32[8,1,262144]{2,1,0:T(1,128)} reshape(f32[2048,32,32]{2,1,0:T(8,128)} %bitcast.60) | data formatting | bytes 16777216
  495.4 100.2 %all_to_all.36 = f32[8,1,262144]{2,1,0:T(1,128)} all-to-all(f32[8,1,262144]{2,1,0:T(1,128)} %reshape.53), channel_id=1, replica_groups=mesh['occ'=8,'vir'=32] {'occ'}, dimensions={0} | all-to-all | bytes 16777216 | tf_op jit(solution)/shard_map/all_to_all | solution.py:63
  595.7 0.5 broadcast.49
  596.2 26.4 %reduce = f32[8,262144]{1,0:T(8,128)} reduce(f32[8,1,262144]{2,1,0:T(1,128)} %all_to_all.36, f32[]{:T(128)} %broadcast.49), dimensions={1}, to_apply=%all_to_all.30.reduce_sub_computation | reduce | bytes 16777220 | tf_op jit(solution)/shard_map/all_to_all | solution.py:63
  622.6 25.3 %reshape.54 = f32[2048,32,32]{2,1,0:T(8,128)} reshape(f32[8,262144]{1,0:T(8,128)} %reduce) | data formatting | bytes 16777216
  647.9 25.1 %copy.10 = f32[8,32,32,256]{3,2,1,0:T(8,128)} copy(f32[8,32,32,256]{2,1,3,0:T(8,128)} %bitcast.61) | data formatting | bytes 16777216 | tf_op jit(solution)/shard_map/all_to_all | solution.py:63
  (18 shorter events, 1.0 us)
Async XLA Ops:
  6.5 6.0 copy-start.1
  6.5 55.7 %all-to-all-start = ((bf16[256,32,256]{2,1,0:T(8,128)(2,1)}), bf16[256,32,256]{2,1,0:T(8,128)(2,1)}, u32[]{:S(2)}, u32[]{:S(2)}) async-start(bf16[256,32,256]{2,1,0:T(8,128)(2,1)} %param.5), calls=%async_computation | async-start | bytes 8388608 | tf_op jit(solution)/shard_map/all_to_all | solution.py:29
  12.5 156.5 %all-reduce.3.cloned.1.call-start = ((), (), s32[]{:S(2)}) async-start(), calls=%async_computation.5 | async-start | bytes 786432 | tf_op jit(solution)/shard_map/psum | solution.py:12
  70.7 99.7 %copy-start.2 = (s32[3]{0:T(128)S(1)}, s32[3]{0:T(128)}, u32[]{:S(2)}) copy-start(s32[3]{0:T(128)} %param.8) | copy-start | bytes 40
  70.7 105.7 %copy-start.3 = (f32[1024]{0:T(1024)S(1)}, f32[1024]{0:T(1024)}, u32[]{:S(2)}) copy-start(f32[1024]{0:T(1024)} %param.7) | copy-start | bytes 12292
  70.7 105.8 %copy-start = (f32[256]{0:T(256)S(1)}, f32[256]{0:T(256)}, u32[]{:S(2)}) copy-start(f32[256]{0:T(256)} %param.6) | copy-start | bytes 3076
  79.9 184.2 %all-gather.4.cloned.1.call-start = ((), (), s32[]{:S(2)}) async-start(), calls=%async_computation.2 | async-start | bytes 4325376 | tf_op jit(solution)/shard_map/all_gather | solution.py:59
  169.0 181.2 %all-gather.6.cloned.1.call-start = ((), (), s32[]{:S(2)}) async-start(), calls=%async_computation.3 | async-start | bytes 4325376 | tf_op jit(solution)/shard_map/all_gather | solution.py:59
  169.8 266.4 %all-gather.8.cloned.1.call-start = ((), (), s32[]{:S(2)}) async-start(), calls=%async_computation.4 | async-start | bytes 4325376 | tf_op jit(solution)/shard_map/all_gather | solution.py:59
Sparse Core Ops, SparseCore 0:
  80.0 88.8 all-reduce.2
  171.8 92.3 all-gather.3
  266.9 83.2 all-gather.5
  352.9 83.2 all-gather.7
where the time goes:
time: 681 us; the launch traced here: 679 us
  waiting for transfers between devices  363 us (53%)
  local copies, waits for them, and re-layouts  120 us (18%)
  blocking collectives  100 us (15%)
  matrix products  36.1 us (5%)
  other arithmetic  28.3 us (4%)
  between operations  25.8 us (4%)
    all_gather x3, waiting for transfers between devices, shards(): lax.all_gather(pair_slabs[step_index], 'vir', axis=0, tiled=True)  231 us
    all_to_all x1, blocking collectives, shards(): lax.all_to_all(density, 'occ', split_axis=2, concat_axis=0, tiled=True)  100 us
    psum x1, waiting for transfers between devices, from_root(): return lax.psum(jnp.where(mine, shard, jnp.zeros_like(shard)), axis)  89 us
    unnamed x10, local copies, waits for them, and re-layouts  45.8 us
    all_to_all x1, waiting for transfers between devices, shards(): lax.all_to_all(factors, 'occ', split_axis=0, concat_axis=2, tiled=True)  41.8 us
    dot_general x3, matrix products, pair_terms(): jnp.einsum('iab,bp->iap', amplitude, column_piece, preferred_element_type...  36.1 us
    all_to_all x1, other arithmetic, shards(): lax.all_to_all(density, 'occ', split_axis=2, concat_axis=0, tiled=True)  26.4 us
    dynamic_update_slice x1, local copies, waits for them, and re-layouts, shards(): lax.dynamic_update_slice_in_dim(density, updated, offsets[step_index], 0)  26.3 us
  transfers between devices with their start and end apart: 5, of which 5 were waited for; matrix products, arithmetic and copies ran while one was open for 4% of the time, Pallas kernels for 0%

commit v1 on v0

--- a/solution.py
+++ b/solution.py
@@ -1,3 +1,4 @@
+import functools
 import jax
 import jax.numpy as jnp
 from jax import lax
@@ -5,6 +6,17 @@
 
 IBK = 16
 STEPS = 3
+
+
+def direct_the_floor(raw, array_dim, which_dim):
+    later = jnp.concatenate(
+        lax.all_to_all(jnp.stack(jnp.split(raw, lax.axis_size("occ"), array_dim)), "occ", 0, 0),
+        which_dim,
+    )
+    return later
+
+
+divide_node = functools.partial(direct_the_floor, array_dim=2, which_dim=0)
 
 
 def from_root(shard, axis, root):
@@ -60,7 +72,7 @@
             e_vir,
         )
         density = lax.dynamic_update_slice_in_dim(density, updated, offsets[step_index], 0)
-    return lax.all_to_all(density, "occ", split_axis=2, concat_axis=0, tiled=True)
+    return divide_node(density)
 
 
 def solution(mesh):

time: 681 us -> 569 us (0.84)
  local copies, waits for them, and re-layouts: 120 us -> 36.5 us
  other arithmetic: 28.3 us -> 1.87 us
    unnamed x10 -> x16, local copies, waits for them, and re-layouts: 45.8 us -> 12.7 us
    all_to_all x1 -> x0, other arithmetic: 26.4 us -> none  [shards(): lax.all_to_all(density, 'occ', split_axis=2, concat_axis=0, tiled=True)]
    dynamic_update_slice x1 -> x0, local copies, waits for them, and re-layouts: 26.3 us -> none  [shards(): lax.dynamic_update_slice_in_dim(density, updated, offsets[step_index], 0)]
    all_to_all x2 -> x0, local copies, waits for them, and re-layouts: 25.6 us -> none  [shards(): lax.all_to_all(density, 'occ', split_axis=2, concat_axis=0, tiled=True)]
  transfers between devices with their start and end apart: 5 -> 5, of which waited for: 5 -> 5; matrix products, arithmetic and copies ran while one was open for 4% -> 5% of each run, Pallas kernels for 0% -> 0%
where the time goes in v1:
time: 569 us; the launch traced here: 568 us
  waiting for transfers between devices  362 us (64%)
  blocking collectives  98.3 us (17%)
  local copies, waits for them, and re-layouts  36.5 us (6%)
  matrix products  36.1 us (6%)
  between operations  26.4 us (5%)
  starting transfers between devices  6.32 us (1%)
    all_gather x3, waiting for transfers between devices, shards(): lax.all_gather(pair_slabs[step_index], 'vir', axis=0, tiled=True)  231 us
    all_to_all x1, blocking collectives, direct_the_floor(): lax.all_to_all(jnp.stack(jnp.split(raw, lax.axis_size('occ'), array_dim))...  98.3 us
    psum x1, waiting for transfers between devices, from_root(): return lax.psum(jnp.where(mine, shard, jnp.zeros_like(shard)), axis)  89 us
    all_to_all x1, waiting for transfers between devices, shards(): lax.all_to_all(factors, 'occ', split_axis=0, concat_axis=2, tiled=True)  41.5 us
    dot_general x3, matrix products, pair_terms(): jnp.einsum('iab,bp->iap', amplitude, column_piece, preferred_element_type...  36.1 us
    all_to_all x2, local copies, waits for them, and re-layouts, shards(): lax.all_to_all(factors, 'occ', split_axis=0, concat_axis=2, tiled=True)  15.9 us
    unnamed x16, local copies, waits for them, and re-layouts  12.7 us
  transfers between devices with their start and end apart: 5, of which 5 were waited for; matrix products, arithmetic and copies ran while one was open for 5% of the time, Pallas kernels for 0%

profile of v1, /device:TPU:1, one launch (start us, length us, event | category | flops | bytes accessed | tf_op | source)
XLA Modules:
  0.0 567.6 jit_solution(8713108653191267978)
XLA Ops:
  6.5 6.0 %all-to-all-start = ((bf16[256,32,256]{2,1,0:T(8,128)(2,1)}), bf16[256,32,256]{2,1,0:T(8,128)(2,1)}, u32[]{:S(2)}, u32[]{:S(2)}) async-start(bf16[256,32,256]{2,1,0:T(8,128)(2,1)} %param.5), calls=%async_computation | async-start | bytes 8388608 | tf_op jit(solution)/shard_map/all_to_all | solution.py:41
  20.7 41.5 %all-to-all-done = bf16[256,32,256]{2,1,0:T(8,128)(2,1)} async-done(((bf16[256,32,256]{2,1,0:T(8,128)(2,1)}), bf16[256,32,256]{2,1,0:T(8,128)(2,1)}, u32[]{:S(2)}, u32[]{:S(2)}) %all-to-all-start) | async-done | bytes 4194336 | tf_op jit(solution)/shard_map/all_to_all | solution.py:41
  62.2 8.5 %copy.8 = bf16[8,32,32,256]{3,0,2,1:T(8,128)(2,1)} copy(bf16[8,32,32,256]{3,2,1,0:T(8,128)(2,1)} %bitcast) | data formatting | bytes 8388608 | tf_op jit(solution)/shard_map/all_to_all | solution.py:41
  70.7 7.4 %all_to_all.19 = bf16[32,32,2048]{2,1,0:T(8,128)(2,1)} reshape(bf16[32,32,8,256]{3,2,1,0:T(8,128)(2,1)} %bitcast.88) | data formatting | bytes 8388608 | tf_op jit(solution)/shard_map/all_to_all | solution.py:41
  78.1 1.8 select_bitcast_fusion
  80.0 89.0 %all-reduce.3.cloned.1.call-done = (bf16[32,2048]{1,0:T(8,128)(2,1)}, bf16[32,2048]{1,0:T(8,128)(2,1)}, bf16[32,2048]{1,0:T(8,128)(2,1)}) async-done(((bf16[32,2048]{1,0:T(8,128)(2,1)}, bf16[32,2048]{1,0:T(8,128)(2,1)}, bf16[32,2048]{1,0:T(8,128)(2,1)}), (bf16[32,2048]{1,0:T(8,128)(2,1)}, bf16[32,2048]{1,0:T(8,128)(2,1)}, bf16[32,2048]{1,0:T(8,128)(2,1)})) %all-reduce.3.cloned.1.call-update) | async-done | bytes 393232 | tf_op jit(solution)/shard_map/psum | solution.py:24
  169.0 0.7 all-gather.6.cloned.1.call-update
  177.5 86.6 %all-gather.4.cloned.1.call-done = bf16[1024,2048]{1,0:T(8,128)(2,1)} async-done(((bf16[32,2048]{1,0:T(8,128)(2,1)}), bf16[1024,2048]{1,0:T(8,128)(2,1)}) %all-gather.4.cloned.1.call-update) | async-done | bytes 4194320 | tf_op jit(solution)/shard_map/all_gather | solution.py:71
  264.1 4.5 broadcast_in_dim.2
  268.6 11.3 %fusion.12 = f32[32,32,2048]{2,1,0:T(8,128)} fusion(f32[32,32,2048]{2,1,0:T(8,128)} %broadcast_in_dim.2, s32[]{:T(128)S(6)} %select_n.99, bf16[1024,2048]{1,0:T(8,128)(2,1)} %all-gather.4.cloned.1.call-done, bf16[32,32,2048]{2,1,0:T(8,128)(2,1)} %all_to_all.19, f32[]{:T(128)} %bitcast.6, f32[16]{0:T(128)S(1)} %get-tuple-element.13, ...), kind=kOutput, calls=%fused_computation.15 | convolution fusion | flops 4297588736 | bytes 14812736 | tf_op jit(solution)/shard_map/iab,bp->iap/dot_general | solution.py:35
  279.8 70.4 %all-gather.6.cloned.1.call-done = bf16[1024,2048]{1,0:T(8,128)(2,1)} async-done(((bf16[32,2048]{1,0:T(8,128)(2,1)}), bf16[1024,2048]{1,0:T(8,128)(2,1)}) %all-gather.6.cloned.1.call-update) | async-done | bytes 4194320 | tf_op jit(solution)/shard_map/all_gather | solution.py:71
  350.2 12.4 %add_dynamic-update-slice_fusion.1 = f32[32,32,2048]{2,1,0:T(8,128)} fusion(f32[32,32,2048]{2,1,0:T(8,128)} %fusion.12, s32[]{:T(128)S(6)} %select_n.109, bf16[1024,2048]{1,0:T(8,128)(2,1)} %all-gather.6.cloned.1.call-done, bf16[32,32,2048]{2,1,0:T(8,128)(2,1)} %all_to_all.19, f32[]{:T(128)} %bitcast.11, f32[16]{0:T(128)S(1)} %get-tuple-element.12, ...), kind=kOutput, calls=%fused_computation.14 | convolution fusion | flops 4298637312 | bytes 19007040 | tf_op jit(solution)/shard_map/iab,bp->iap/dot_general | solution.py:35
  362.6 73.5 %all-gather.8.cloned.1.call-done = bf16[1024,2048]{1,0:T(8,128)(2,1)} async-done(((bf16[32,2048]{1,0:T(8,128)(2,1)}), bf16[1024,2048]{1,0:T(8,128)(2,1)}) %all-gather.8.cloned.1.call-update) | async-done | bytes 4194320 | tf_op jit(solution)/shard_map/all_gather | solution.py:71
  436.1 12.5 %add_dynamic-update-slice_fusion = f32[32,32,2048]{2,1,0:T(8,128)} fusion(f32[32,32,2048]{2,1,0:T(8,128)} %add_dynamic-update-slice_fusion.1, s32[]{:T(128)S(6)} %select_n.118, bf16[1024,2048]{1,0:T(8,128)(2,1)} %all-gather.8.cloned.1.call-done, bf16[32,32,2048]{2,1,0:T(8,128)(2,1)} %all_to_all.19, f32[]{:T(128)} %bitcast.16, f32[16]{0:T(128)S(1)} %get-tuple-element.11, ...), kind=kOutput, calls=%fused_computation.13 | convolution fusion | flops 4298637312 | bytes 19007040 | tf_op jit(solution)/shard_map/iab,bp->iap/dot_general | solution.py:35
  448.6 1.3 fusion.53
  450.0 1.3 fusion.52
  451.3 1.3 fusion.51
  452.7 1.3 fusion.50
  454.0 1.3 fusion.49
  455.3 1.3 fusion.48
  456.7 1.3 fusion.47
  458.0 1.3 fusion.46
  459.3 98.3 %all_to_all.23 = f32[8,32,32,256]{3,2,1,0:T(8,128)S(1)} all-to-all(f32[8,32,32,256]{3,2,1,0:T(8,128)S(1)} %fusion.46), channel_id=1, replica_groups=mesh['occ'=8,'vir'=32] {'occ'}, dimensions={0} | all-to-all | bytes 16777216 | tf_op jit(solution)/shard_map/all_to_all | solution.py:13
  557.6 3.4 copy.23
  (21 shorter events, 2.9 us)
Async XLA Ops:
  6.5 6.0 %copy-start.1 = (s32[3]{0:T(128)S(1)}, s32[3]{0:T(128)}, u32[]{:S(2)}) copy-start(s32[3]{0:T(128)} %param.9) | copy-start | bytes 40
  6.5 55.7 %all-to-all-start = ((bf16[256,32,256]{2,1,0:T(8,128)(2,1)}), bf16[256,32,256]{2,1,0:T(8,128)(2,1)}, u32[]{:S(2)}, u32[]{:S(2)}) async-start(bf16[256,32,256]{2,1,0:T(8,128)(2,1)} %param.5), calls=%async_computation | async-start | bytes 8388608 | tf_op jit(solution)/shard_map/all_to_all | solution.py:41
  12.5 156.5 %all-reduce.3.cloned.1.call-start = ((), (), s32[]{:S(2)}) async-start(), calls=%async_computation.5 | async-start | bytes 786432 | tf_op jit(solution)/shard_map/psum | solution.py:24
  70.7 99.6 %copy-start.2 = (s32[3]{0:T(128)S(1)}, s32[3]{0:T(128)}, u32[]{:S(2)}) copy-start(s32[3]{0:T(128)} %param.8) | copy-start | bytes 40
  70.7 105.9 %copy-start.3 = (f32[1024]{0:T(1024)S(1)}, f32[1024]{0:T(1024)}, u32[]{:S(2)}) copy-start(f32[1024]{0:T(1024)} %param.7) | copy-start | bytes 12292
  70.7 106.0 %copy-start = (f32[256]{0:T(256)S(1)}, f32[256]{0:T(256)}, u32[]{:S(2)}) copy-start(f32[256]{0:T(256)} %param.6) | copy-start | bytes 3076
  79.9 184.2 %all-gather.4.cloned.1.call-start = ((), (), s32[]{:S(2)}) async-start(), calls=%async_computation.2 | async-start | bytes 4325376 | tf_op jit(solution)/shard_map/all_gather | solution.py:71
  169.0 181.2 %all-gather.6.cloned.1.call-start = ((), (), s32[]{:S(2)}) async-start(), calls=%async_computation.3 | async-start | bytes 4325376 | tf_op jit(solution)/shard_map/all_gather | solution.py:71
  169.7 266.4 %all-gather.8.cloned.1.call-start = ((), (), s32[]{:S(2)}) async-start(), calls=%async_computation.4 | async-start | bytes 4325376 | tf_op jit(solution)/shard_map/all_gather | solution.py:71
Sparse Core Ops, SparseCore 0:
  80.0 88.8 all-reduce.2
  171.8 92.3 all-gather.3
  266.9 83.2 all-gather.5
  352.8 83.2 all-gather.7
